TPU v7x, 256 devices: a whole 4x4x8 slice. The times are simulated.
256 devices in a mesh: leaf: 16 (over z, core), prow: 4 (over x), pcol: 4 (over y).
Axes of the slice: x: 4, y: 4, z: 8, core: 2. Of those that a mesh axis runs over, the one named last changes fastest.
Arguments:
- child_inverse: float32 [256, 512, 512], P(('leaf', 'prow', 'pcol')), parts along dimension 0, as said below
- child_coupling: float32 [256, 1024, 512], P(('leaf', 'prow', 'pcol')), parts along dimension 0, may hold values from -0.25 to 0.25
- child_blocks: int32 [256], P(('leaf', 'prow', 'pcol')), parts along dimension 0, may hold values from 2 to 8, as said below
- child_map: int32 [256, 8], P(('leaf', 'prow', 'pcol')), parts along dimension 0, may hold values from -1 to 15, as said below
- parent_front: float32 [32768, 2048], P(('leaf', 'prow'), 'pcol'), parts along dimension 0, as said below
Outputs:
- parent_factored: float32 [32768, 2048], P(('leaf', 'prow'), 'pcol'), parts along dimension 0
There are 16 independent parts, one for each index of `leaf`. A program takes and returns all parts, laid end to end along the dimension named above; each array names one. Nothing has to cross between parts.
Inputs may be any that keep to these rules, and one draw needn't show every extreme that they name: `child_inverse`: each matrix is lower triangular with a positive diagonal. `child_blocks`: the largest value 8 is taken by some child in every draw. `child_map`: in row c the first child_blocks[c] entries are distinct parent block ids in increasing order and the others are -1. `parent_front`: symmetric; the assembled front is positive definite.
All inputs are finite; a program needn't handle non-finite values.
Results may differ from a plain program's by a relative error of at most 0.0003.
Values sent between devices are 32-bit elements; how exact they have to be, the bound alone decides.
A program may use at most 128 MiB of HBM per device.

v0:
```python
import jax
import jax.numpy as jnp
from jax import lax
from jax.sharding import PartitionSpec as P

SMAX = 1024
BLK = 128
PORD = 2048


def spread_2(value, axis, root):
    mine = lax.axis_index(axis) == root
    return lax.psum(jnp.where(mine, value, jnp.zeros_like(value)), axis)


def factor_child(inverse_block, coupling, blocks):
    row_ids = jnp.arange(coupling.shape[0])
    masked = jnp.where((row_ids < blocks * BLK)[:, None], coupling, jnp.zeros_like(coupling))
    return jnp.dot(
        masked, inverse_block.T, precision=lax.Precision.HIGHEST, preferred_element_type=jnp.float32
    )


def selection(mapping, block_total):
    return (mapping[None, :] == jnp.arange(block_total)[:, None]).astype(jnp.float32)


def body(child_inverse, child_coupling, child_blocks, child_map, parent_front):
    row_index = lax.axis_index("prow")
    col_index = lax.axis_index("pcol")
    row_count = lax.axis_size("prow")
    col_count = lax.axis_size("pcol")
    tile_rows = parent_front.shape[0]
    tile_cols = parent_front.shape[1]
    slot_count = SMAX // BLK
    block_total = PORD // BLK
    factors = jax.vmap(factor_child)(child_inverse, child_coupling, child_blocks)
    factor = factors[0]
    update = jnp.einsum(
        "ip,jp->ij",
        factor,
        factor,
        precision=lax.Precision.HIGHEST,
        preferred_element_type=jnp.float32,
    )
    select = selection(child_map[0], block_total)
    by_row = select.reshape(row_count, block_total // row_count, slot_count)
    by_col = select.reshape(col_count, block_total // col_count, slot_count)
    blocked = update.reshape(slot_count, BLK, slot_count, BLK)
    spread = jnp.einsum(
        "rbk,kiln,cdl->rcbidn", by_row, blocked, by_col, precision=lax.Precision.HIGHEST
    )
    child_sums = spread.reshape(row_count * col_count, tile_rows, tile_cols)
    received = lax.psum_scatter(child_sums, ("prow", "pcol"), scatter_dimension=0, tiled=True)
    contribution = received[0]
    assembled = parent_front - contribution
    column = spread_2(assembled, "pcol", 0)
    full_column = lax.all_gather(column, "prow", axis=0, tiled=True)
    diag_factor = jnp.linalg.cholesky(full_column[:tile_rows])
    solved = lax.linalg.triangular_solve(
        diag_factor, full_column, left_side=False, lower=True, transpose_a=True
    )
    panel_rows = jnp.concatenate([diag_factor, solved[tile_rows:]], 0)
    own_panel = lax.dynamic_slice_in_dim(panel_rows, row_index * tile_rows, tile_rows, 0)
    col_panel = lax.dynamic_slice_in_dim(panel_rows, col_index * tile_cols, tile_cols, 0)
    product = jnp.einsum(
        "ip,jp->ij",
        own_panel,
        col_panel,
        precision=lax.Precision.HIGHEST,
        preferred_element_type=jnp.float32,
    )
    global_rows = row_index * tile_rows + jnp.arange(tile_rows)
    global_cols = col_index * tile_cols + jnp.arange(tile_cols)
    padded = jnp.concatenate(
        [own_panel, jnp.zeros((tile_rows, tile_cols - tile_rows), jnp.float32)], 1
    )
    trailing = jnp.where(global_rows[:, None] >= tile_rows, assembled - product, assembled)
    return jnp.where(global_cols[None, :] < tile_rows, padded, trailing)


def solution(mesh):
    return jax.shard_map(
        body,
        mesh=mesh,
        in_specs=(
            P(("leaf", "prow", "pcol"), None, None),
            P(("leaf", "prow", "pcol"), None, None),
            P(("leaf", "prow", "pcol")),
            P(("leaf", "prow", "pcol"), None),
            P(("leaf", "prow"), "pcol"),
        ),
        out_specs=P(("leaf", "prow"), "pcol"),
        check_vma=False,
    )
```

profile of v0, /device:TPU:1, one launch (start us, length us, event | category | flops | bytes accessed | tf_op | source)
XLA Modules:
  0.0 483.2 jit_solution(5577353358900809291)
XLA Ops:
  7.3 1.8 broadcast_select_fusion
  9.1 3.5 convolution_bitcast_fusion.1
  12.6 8.2 %fusion.13 = f32[8,128,8,128]{3,0,2,1:T(8,128)S(1)} fusion(f32[8,128,512,1]{2,1,0,3:T(8,128)S(1)} %convolution_bitcast_fusion.1), kind=kOutput, calls=%fused_computation.18 | convolution fusion | flops 6442450944 | bytes 6291456 | tf_op jit(solution)/shard_map/ip,jp->ij/dot_general | solution.py:39
  20.8 7.4 %convolution_bitcast_fusion = f32[128,8,128,4,4,1]{2,4,3,1,0,5:T(4,128)S(1)} fusion(f32[8,128,8,128]{3,0,2,1:T(8,128)S(1)} %fusion.13, s32[4,4]{1,0:T(4,128)S(1)} %multiply_add_fusion, s32[8]{0:T(128)S(1)} %bitcast.86), kind=kOutput, calls=%fused_computation.5 | convolution fusion | flops 201326720 | bytes 12583008 | tf_op jit(solution)/shard_map/rbk,kiln,cdl->rcbidn/dot_general | solution.py:50
  28.3 15.9 %fusion.2 = f32[4,4,4,128,4,128]{5,4,1,2,0,3:T(4,128)} fusion(f32[128,8,128,4,4,1]{2,4,3,1,0,5:T(4,128)S(1)} %convolution_bitcast_fusion, s32[4,4]{1,0:T(4,128)S(1)} %multiply_add_fusion, s32[8]{0:T(128)S(1)} %bitcast.87), kind=kOutput, calls=%fused_computation.4 | convolution fusion | flops 402653312 | bytes 25165920 | tf_op jit(solution)/shard_map/rbk,kiln,cdl->rcbidn/dot_general | solution.py:50
  44.2 19.8 %copy.64 = f32[4,4,4,128,4,128]{3,2,5,4,1,0:T(4,128)} copy(f32[4,4,4,128,4,128]{5,4,1,2,0,3:T(4,128)} %fusion.2) | data formatting | bytes 33554432 | tf_op jit(solution)/shard_map/reshape | solution.py:53
  64.0 19.9 %reshape.115 = f32[16,512,512]{1,2,0:T(8,128)} reshape(f32[4,4,4,128,4,128]{3,2,5,4,1,0:T(4,128)} %copy.64) | data formatting | bytes 33554432 | tf_op jit(solution)/shard_map/reshape | solution.py:53
  84.0 1.1 copy-done.4
  85.1 0.3 copy.35
  85.5 117.8 %reduce-scatter.4.cloned.1.call-done = f32[1,512,512]{1,2,0:T(8,128)} async-done(((f32[16,512,512]{1,2,0:T(8,128)}), f32[1,512,512]{1,2,0:T(8,128)}) %reduce-scatter.4.cloned.1.call-update) | async-done | bytes 1048592
  203.3 2.4 broadcast_select_fusion.1
  205.7 0.4 all-gather.2.cloned.1.call-start
  206.2 48.9 %all-reduce.4.cloned.1.call-done = f32[512,512]{0,1:T(8,128)} async-done(((f32[512,512]{0,1:T(8,128)}), f32[512,512]{0,1:T(8,128)}) %all-reduce.4.cloned.1.call-update) | async-done | bytes 1048592 | tf_op jit(solution)/shard_map/psum | solution.py:13
  255.1 0.5 iota_multiply_fusion
  255.6 54.6 %all-gather.2.cloned.1.call-done = f32[2048,512]{0,1:T(8,128)} async-done(((f32[512,512]{0,1:T(8,128)}), f32[2048,512]{0,1:T(8,128)}) %all-gather.2.cloned.1.call-update) | async-done | bytes 4194320 | tf_op jit(solution)/shard_map/all_gather | solution.py:58
  310.2 1.3 slice.122
  311.5 0.3 copy.36
  311.9 1.4 fusion.24
  313.3 11.7 %cholesky.103 = f32[128,128]{1,0:T(8,128)S(1)} custom-call(f32[128,128]{1,0:T(8,128)S(1)} %cholesky.263), custom_call_target="Cholesky" | custom-call | tf_op jit(solution)/shard_map/jit(cholesky)/cholesky | solution.py:59
  325.1 9.8 %custom-call.30 = f32[1,128,128]{1,2,0:T(8,128)S(1)} custom-call(f32[1,128,128]{2,1,0:T(8,128)S(1)} %get-tuple-element.42), custom_call_target="InvertDiagBlocksLowerTriangular" | custom-call | tf_op jit(solution)/shard_map/jit(cholesky)/cholesky | solution.py:59
  334.9 0.3 fusion.32
  335.2 0.3 convolution_subtract_fusion.2
  335.6 11.7 %cholesky.215 = f32[128,128]{1,0:T(8,128)S(1)} custom-call(f32[128,128]{1,0:T(8,128)S(1)} %cholesky.267), custom_call_target="Cholesky" | custom-call | tf_op jit(solution)/shard_map/jit(cholesky)/cholesky | solution.py:59
  347.3 0.7 copy.39
  348.2 0.7 copy.37
  348.9 10.6 %custom-call.31 = f32[1,128,128]{1,2,0:T(8,128)} custom-call(f32[1,128,128]{2,1,0:T(8,128)S(1)} %get-tuple-element.40), custom_call_target="InvertDiagBlocksLowerTriangular" | custom-call | tf_op jit(solution)/shard_map/jit(cholesky)/cholesky | solution.py:59
  359.5 1.0 cholesky.222
  360.5 0.8 constant_dynamic-update-slice_fusion.2
  361.3 1.2 convolution_dynamic-update-slice_fusion
  362.5 0.6 convolution_subtract_fusion.3
  363.1 11.7 %cholesky.236 = f32[128,128]{1,0:T(8,128)S(1)} custom-call(f32[128,128]{1,0:T(8,128)S(1)} %cholesky.272), custom_call_target="Cholesky" | custom-call | tf_op jit(solution)/shard_map/jit(cholesky)/cholesky | solution.py:59
  374.9 9.8 %custom-call.32 = f32[1,128,128]{1,2,0:T(8,128)S(1)} custom-call(f32[1,128,128]{2,1,0:T(8,128)S(1)} %get-tuple-element.38), custom_call_target="InvertDiagBlocksLowerTriangular" | custom-call | tf_op jit(solution)/shard_map/jit(cholesky)/cholesky | solution.py:59
  385.0 0.5 convolution_subtract_fusion.4
  385.5 11.9 %cholesky.253 = f32[128,128]{1,0:T(8,128)S(1)} custom-call(f32[128,128]{1,0:T(8,128)S(1)} %convolution_subtract_fusion.4), custom_call_target="Cholesky" | custom-call | tf_op jit(solution)/shard_map/jit(cholesky)/cholesky | solution.py:59
  397.6 0.6 compare_reduce_fusion.1
  398.2 0.7 compare_reduce_fusion
  398.9 0.7 compare_reduce_fusion.2
  402.2 1.2 fusion.28
  403.4 0.6 triangular_solve.75
  404.0 14.2 %while.1 = (s32[]{:T(128)}, f32[512,512]{0,1:T(8,128)}, s32[4,2]{0,1:T(2,128)S(1)}, f32[4,128,128]{2,1,0:T(8,128)}, s32[]{:T(128)}) while((s32[]{:T(128)}, f32[512,512]{0,1:T(8,128)}, s32[4,2]{0,1:T(2,128)S(1)}, f32[4,128,128]{2,1,0:T(8,128)}, s32[]{:T(128)}) %tuple.27), condition=%wide.while_cond, body=%wide.while_body.sunk | while | flops 2 | bytes 393829 | solution.py:60
  404.0 0.5 fusion.62
  404.6 2.2 dynamic-slice.9
  406.9 0.6 bitcast_dynamic-update-slice_fusion.2
  407.6 0.5 fusion.62
  408.2 2.2 dynamic-slice.9
  410.5 0.6 bitcast_dynamic-update-slice_fusion.2
  411.2 0.5 fusion.62
  411.7 2.2 dynamic-slice.9
  414.1 0.6 bitcast_dynamic-update-slice_fusion.2
  414.8 0.5 fusion.62
  415.3 2.2 dynamic-slice.9
  417.6 0.6 bitcast_dynamic-update-slice_fusion.2
  418.2 40.1 %custom-call.33 = f32[4,128,128]{1,2,0:T(8,128)S(1)} custom-call(f32[4,128,128]{2,1,0:T(8,128)} %get-tuple-element.12), custom_call_target="InvertDiagBlocksLowerTriangular" | custom-call | tf_op jit(solution)/shard_map/triangular_solve | solution.py:60
  458.3 2.4 fusion.22
  460.8 2.3 convolution_subtract_fusion.1
  463.1 1.1 fusion.39
  464.2 2.2 convolution_subtract_fusion
  466.5 1.1 fusion.38
  467.6 3.2 fusion.15
  470.7 1.1 fusion.37
  471.8 0.9 fusion.5
  472.7 0.3 copy-done.3
  473.1 1.9 fusion.21
  475.0 1.3 copy.49
  (42 shorter events, 1.6 us)
Async XLA Ops:
  6.5 2.6 copy-start
  6.5 196.7 %reduce-scatter.4.cloned.1.call-start = ((), (), s32[]{:S(2)}) async-start(), calls=%async_computation.3 | async-start | bytes 17825792
  12.6 8.2 %copy-start.5 = (s32[1,8]{1,0:T(1,128)S(1)}, s32[1,8]{1,0:T(1,128)}, u32[]{:S(2)}) copy-start(s32[1,8]{1,0:T(1,128)} %param.8) | copy-start | bytes 100
  83.9 1.2 copy-start.4
  83.9 171.1 %all-reduce.4.cloned.1.call-start = ((), (), s32[]{:S(2)}) async-start(), calls=%async_computation.1 | async-start | bytes 2097152 | tf_op jit(solution)/shard_map/psum | solution.py:13
  205.7 104.5 %all-gather.2.cloned.1.call-start = ((), (), s32[]{:S(2)}) async-start(), calls=%async_computation.2 | async-start | bytes 5242880 | tf_op jit(solution)/shard_map/all_gather | solution.py:58
  458.3 5.9 %copy-start.2 = (f32[2048,512]{0,1:T(8,128)S(1)}, f32[2048,512]{0,1:T(8,128)}, u32[]{:S(2)}) copy-start(f32[2048,512]{0,1:T(8,128)} %all-gather.2.cloned.1.call-done) | copy-start | bytes 12582916
  471.8 1.2 copy-start.3
  471.8 4.5 copy-start.1
Sparse Core Ops, SparseCore 0:
  84.0 119.1 reduce-scatter.3
  205.8 49.1 all-reduce.3
  256.9 53.3 all-gather.1
where the time goes:
time: 493 us; the launch traced here: 483 us
  waiting for transfers between devices  221 us (45%)
  other arithmetic  128 us (26%)
  local copies, waits for them, and re-layouts  62.9 us (13%)
  matrix products  53.5 us (11%)
  between operations  17.1 us (3%)
    unnamed x4, waiting for transfers between devices  118 us
    another operation x14, other arithmetic, body(): diag_factor = jnp.linalg.cholesky(full_column[:tile_rows])  79.4 us
    all_gather x1, waiting for transfers between devices, body(): full_column = lax.all_gather(column, 'prow', axis=0, tiled=True)  54.6 us
    psum x1, waiting for transfers between devices, spread_2(): return lax.psum(jnp.where(mine, value, jnp.zeros_like(value)), axis)  48.9 us
    another operation x3, other arithmetic, body(): lax.linalg.triangular_solve(diag_factor, full_column, left_side=False, lo...  41.8 us
    reshape x2, local copies, waits for them, and re-layouts, body(): child_sums = spread.reshape(row_count * col_count, tile_rows, tile_cols)  39.7 us
    dot_general x2, matrix products, body(): jnp.einsum('rbk,kiln,cdl->rcbidn', by_row, blocked, by_col, precision=lax...  23.3 us
    another operation x20, local copies, waits for them, and re-layouts  14.2 us
  transfers between devices with their start and end apart: 3, of which 3 were waited for; matrix products, arithmetic and copies ran while one was open for 0% of the time, Pallas kernels for 0%

commit v1 on v0

v1 whole, which is shorter than its diff:
```python
import functools

import jax
import jax.numpy as jnp
from jax import lax
from jax.experimental import pallas as pl
from jax.experimental.pallas import tpu as pltpu
from jax.sharding import PartitionSpec as P

BLK = 128
TILE = 512
NT = 10
GROUPS = ((0, 1), (1, 3), (4, 3), (7, 3))
OWNERS = ((1, 1), (2, 1), (3, 1), (2, 2), (3, 2), (3, 3))
AXES = ("prow", "pcol")
F32 = jnp.float32
BF16 = jnp.bfloat16
DN_NT = (((1,), (1,)), ((), ()))


def split(x):
    hi = x.astype(BF16)
    return hi, (x - hi.astype(F32)).astype(BF16)


def dot_nt(a, b):
    return lax.dot_general(a, b, DN_NT, preferred_element_type=F32)


def dot3(a, b):
    return dot_nt(a[0], b[0]) + dot_nt(a[0], b[1]) + dot_nt(a[1], b[0])


def mm_nt(a, b):
    return dot3(split(a), split(b))


def kernel(slot_ref, inv_ref, coup_ref, parent_ref, out_ref,
           fac_h, fac_l, fh, fl, s_buf, rl1, rf1, rl2, rf2, w_buf, z_buf, t_buf,
           ch, md, linv, p_buf,
           send_sem, recv_sem, dist_send, dist_recv):
    ci = lax.axis_index("prow")
    cj = lax.axis_index("pcol")
    coord = {"prow": ci, "pcol": cj}

    def nxt(v, k):
        return lax.rem(v + k, 4)

    barrier = pltpu.get_barrier_semaphore()
    for dx in range(4):
        for dy in range(4):
            if dx or dy:
                pl.semaphore_signal(
                    barrier, inc=1,
                    device_id={"prow": nxt(ci, dx), "pcol": nxt(cj, dy)},
                    device_id_type=pl.DeviceIdType.MESH)

    ih, il = split(inv_ref[...])

    @pl.loop(0, 8)
    def _(s):
        c = split(coup_ref[pl.ds(pl.multiple_of(s * BLK, BLK), BLK), :])
        f = dot3(c, (ih, il))
        h, l = split(f)
        fac_h[s] = h
        fac_l[s] = l

    @pl.loop(0, 16)
    def _(b):
        s = slot_ref[b]
        ok = slot_ref[16 + b] > 0
        h = fac_h[s]
        l = fac_l[s]
        rows = pl.ds(pl.multiple_of(b * BLK, BLK), BLK)
        fh[rows, :] = jnp.where(ok, h, jnp.zeros_like(h))
        fl[rows, :] = jnp.where(ok, l, jnp.zeros_like(l))

    def tile(r, col, t):
        rows = pl.ds(pl.multiple_of(r * TILE, TILE), TILE)
        cols = pl.ds(col * TILE, TILE)
        d = dot3((fh[rows, :], fl[rows, :]), (fh[cols, :], fl[cols, :]))
        if col == 0:
            mine = jnp.logical_and(ci == r, cj == 0)
            d = d - jnp.where(mine, parent_ref[...], jnp.zeros((TILE, TILE), F32))
        for c in range(2):
            for a in range(4):
                o = c * 256 + a * 64
                s_buf[c, a, t] = d[o:o + 64]

    def tiles(col, lo, hi, base):
        @pl.loop(lo, hi)
        def _(r):
            tile(r, col, base + r)

    def copy(src, dst, g, c, d, kind, axis, k):
        return pltpu.make_async_remote_copy(
            src_ref=src, dst_ref=dst,
            send_sem=send_sem.at[g, c, d, kind], recv_sem=recv_sem.at[g, c, d, kind],
            device_id={axis: nxt(coord[axis], k)}, device_id_type=pl.DeviceIdType.MESH)

    started = []

    def go(cp):
        cp.start()
        started.append(cp)

    STEP = (1, 3)

    def rs(g, c, phase):
        t0, n = GROUPS[g]
        ts = pl.ds(t0, n)
        first, second = AXES[c], AXES[1 - c]
        m = coord[first]
        if phase == 1:
            axis, me, half = first, m, 32
            rl, rf, kb = rl1, rf1, 0

            def chunk(d, h):
                return s_buf.at[c, d, ts, pl.ds(h * 32, 32)]
        else:
            axis, me, half = second, coord[second], 8
            rl, rf, kb = rl2, rf2, 3

            def chunk(d, h):
                return s_buf.at[c, m, ts, pl.ds(pl.multiple_of(d * 16 + h * 8, 8), 8)]
        relay = [copy(chunk(nxt(me, 2), 1 - d), rl.at[c, d, ts], g, c, d, kb, axis, STEP[d])
                 for d in range(2)]
        raw = [copy(chunk(nxt(me, STEP[d]), d), rf.at[c, d, ts, pl.ds(d * half, half)], g, c, d, kb + 1, axis, STEP[d])
               for d in range(2)]
        fin = [copy(chunk(nxt(me, STEP[d]), 1 - d), rf.at[c, d, ts, pl.ds((1 - d) * half, half)], g, c, d, kb + 2, axis, STEP[d])
               for d in range(2)]
        return relay, raw, fin, chunk, me, rl, rf

    def rs_start(g, phase):
        for c in range(2):
            relay, raw, *_ = rs(g, c, phase)
            for d in range(2):
                go(relay[d])
            for d in range(2):
                go(raw[d])

    def rs_relay(g, phase):
        t0, n = GROUPS[g]
        for c in range(2):
            relay, raw, fin, chunk, me, rl, rf = rs(g, c, phase)
            for d in range(2):
                relay[d].wait_recv()
                ref = chunk(nxt(me, STEP[d]), 1 - d)
                ref[...] = ref[...] + rl[c, d, t0:t0 + n]
                go(fin[d])

    def rs_final(g, phase):
        t0, n = GROUPS[g]
        for c in range(2):
            relay, raw, fin, chunk, me, rl, rf = rs(g, c, phase)
            for d in range(2):
                raw[d].wait_recv()
                fin[d].wait_recv()
            m = coord[AXES[c]]
            if phase == 1:
                for t in range(t0, t0 + n):
                    s_buf[c, m, t] = s_buf[c, m, t] + rf[c, 0, t] + rf[c, 1, t]
            else:
                rows = pl.ds(pl.multiple_of(me * 16, 16), 16)
                for t in range(t0, t0 + n):
                    z = s_buf[c, m, t, rows, :] + rf[c, 0, t] + rf[c, 1, t]
                    if g < 2:
                        w_buf[c, m, t, rows, :] = z
                    else:
                        z_buf[c, t - 4] = z

    def ag(g, c, phase):
        t0, n = GROUPS[g]
        ts = pl.ds(t0, n)
        first, second = AXES[c], AXES[1 - c]
        m = coord[first]
        if phase == 3:
            axis, me, kb = second, coord[second], 6

            def part(v, h, k):
                return w_buf.at[c, m, ts, pl.ds(pl.multiple_of(v * 16 + h * 8, 8), k * 8)]
        else:
            axis, me, kb = first, m, 8

            def part(v, h, k):
                return w_buf.at[c, v, ts, pl.ds(h * 32, k * 32)]
        own = []
        own_in = []
        fwd = []
        fwd_in = []
        for d in range(2):
            src = part(me, 0, 2)
            own.append(copy(src, src, g, c, d, kb, axis, STEP[d]))
            inc = part(nxt(me, STEP[1 - d]), 0, 2)
            own_in.append(copy(inc, inc, g, c, d, kb, axis, STEP[d]))
            f = part(nxt(me, STEP[1 - d]), d, 1)
            fwd.append(copy(f, f, g, c, d, kb + 1, axis, STEP[d]))
            fi = part(nxt(me, 2), d, 1)
            fwd_in.append(copy(fi, fi, g, c, d, kb + 1, axis, STEP[d]))
        return own, own_in, fwd, fwd_in

    def ag_start(g, phase):
        for c in range(2):
            for cp in ag(g, c, phase)[0]:
                go(cp)

    def ag_forward(g, phase):
        for c in range(2):
            own, own_in, fwd, fwd_in = ag(g, c, phase)
            for d in range(2):
                own_in[d].wait_recv()
                go(fwd[d])

    def ag_final(g, phase):
        for c in range(2):
            own, own_in, fwd, fwd_in = ag(g, c, phase)
            for d in range(2):
                fwd_in[d].wait_recv()

    deliveries = []

    def deliver(g):
        t0, n = GROUPS[g]
        for t in range(t0 - 4, t0 - 4 + n):
            r, q = OWNERS[t]
            for k, (x, y) in enumerate(((r, q), (q, r))[: 1 if r == q else 2]):
                mine = jnp.logical_and(ci == x, cj == y)
                for c in range(2):
                    m = coord[AXES[c]]
                    v = coord[AXES[1 - c]]
                    rows = pl.ds(pl.multiple_of(c * 256 + m * 64 + v * 16, 16), 16)
                    cp = pltpu.make_async_remote_copy(
                        src_ref=z_buf.at[c, t], dst_ref=t_buf.at[rows],
                        send_sem=dist_send.at[t, k, c], recv_sem=dist_recv.at[0],
                        device_id={"prow": x, "pcol": y}, device_id_type=pl.DeviceIdType.MESH)

                    @pl.when(mine)
                    def _():
                        t_buf[rows, :] = z_buf[c, t]

                    @pl.when(jnp.logical_not(mine))
                    def _():
                        cp.start()
                    deliveries.append((mine, cp))

    def chol_begin(kb):
        o = kb * BLK
        eye = lax.broadcasted_iota(jnp.int32, (BLK, BLK), 0) == lax.broadcasted_iota(jnp.int32, (BLK, BLK), 1)
        md[:, 0:BLK] = ch[o:o + BLK, o:o + BLK]
        md[:, BLK:2 * BLK] = eye.astype(F32)

    def chol_chunk(q):
        lo = q * 32
        x = md[lo:BLK, 0:BLK]
        y = md[lo:BLK, BLK:2 * BLK]
        rid = lax.broadcasted_iota(jnp.int32, (BLK - lo, BLK), 0)
        for k in range(32):
            row = x[k:k + 1, :]
            col = jnp.broadcast_to(x[:, lo + k:lo + k + 1], x.shape)
            piv = col[k:k + 1, :]
            inv = 1.0 / piv
            mul = jnp.where(rid > k, col, 0.0)
            x = x - mul * (row * inv)
            y = y - mul * (y[k:k + 1, :] * inv)
        md[lo:BLK, 0:BLK] = x
        md[lo:BLK, BLK:2 * BLK] = y

    def chol_end(kb):
        o = kb * BLK
        ri = lax.broadcasted_iota(jnp.int32, (BLK, BLK), 0)
        cj_ = lax.broadcasted_iota(jnp.int32, (BLK, BLK), 1)
        u = md[:, 0:BLK]
        piv = jnp.sum(jnp.where(ri == cj_, u, 0.0), axis=1, keepdims=True)
        sc = lax.rsqrt(piv)
        li = md[:, BLK:2 * BLK] * sc
        linv[kb] = li
        low = jnp.where(cj_ >= ri, u * sc, 0.0).T
        ch[o:o + BLK, o:o + BLK] = low
        if kb < 3:
            lp = lax.dot_general(ch[o + BLK:, o:o + BLK], li, DN_NT, precision=lax.Precision.HIGHEST,
                                 preferred_element_type=F32)
            ch[o + BLK:, o:o + BLK] = lp
            ch[o + BLK:, o + BLK:] = ch[o + BLK:, o + BLK:] - lax.dot_general(
                lp, lp, DN_NT, precision=lax.Precision.HIGHEST, preferred_element_type=F32)
            ch[o:o + BLK, o + BLK:] = jnp.zeros((BLK, TILE - o - BLK), F32)

    def solve(x, idx):
        @pl.loop(0, 2)
        def _(c):
            a = -jnp.reshape(w_buf[c, :, pl.ds(idx, 1)], (256, TILE))
            rows = pl.ds(pl.multiple_of(c * 256, 256), 256)
            for b in range(4):
                o = b * BLK
                v = a[:, o:o + BLK]
                if b:
                    v = v - mm_nt(p_buf[x, rows, 0:o], ch[o:o + BLK, 0:o])
                p_buf[x, rows, o:o + BLK] = mm_nt(v, linv[b])

    tiles(0, 0, 1, 0)
    pl.semaphore_wait(barrier, 15)
    rs_start(0, 1)
    tiles(0, 1, 4, 0)
    rs_start(1, 1)
    rs_relay(0, 1)
    rs_final(0, 1)
    rs_start(0, 2)
    tiles(1, 1, 4, 3)
    rs_relay(0, 2)
    rs_relay(1, 1)
    rs_final(0, 2)
    ag_start(0, 3)
    rs_start(2, 1)
    ag_forward(0, 3)
    ag_final(0, 3)
    ag_start(0, 4)
    rs_final(1, 1)
    rs_start(1, 2)
    ag_forward(0, 4)
    tiles(2, 2, 4, 5)
    tiles(3, 3, 4, 6)
    rs_relay(1, 2)
    rs_relay(2, 1)
    ag_final(0, 4)
    for c in range(2):
        for a in range(4):
            o = c * 256 + a * 64
            ch[o:o + 64, :] = -w_buf[c, a, 0]

    def chol(kb, events):
        chol_begin(kb)
        for q in range(4):
            chol_chunk(q)
            for e in events[q]:
                e()
        chol_end(kb)

    P_ = functools.partial
    rs_final(1, 2)
    ag_start(1, 3)
    rs_start(3, 1)
    chol(0, ((P_(ag_forward, 1, 3), P_(ag_final, 1, 3), P_(ag_start, 1, 4)),
             (P_(rs_final, 2, 1), P_(rs_start, 2, 2)),
             (P_(rs_relay, 2, 2), P_(rs_relay, 3, 1)),
             (P_(ag_forward, 1, 4),)))
    chol(1, ((P_(rs_final, 2, 2), P_(deliver, 2)),
             (P_(rs_final, 3, 1), P_(rs_start, 3, 2)),
             (P_(rs_relay, 3, 2),),
             (P_(rs_final, 3, 2), P_(deliver, 3))))
    chol(2, ((), (), (), ()))
    chol(3, ((), (), (), ()))
    ag_final(1, 4)

    trail = jnp.logical_and(ci > 0, cj > 0)

    @pl.when(ci > 0)
    def _():
        solve(0, ci)

    @pl.when(trail)
    def _():
        solve(1, cj)

        @pl.loop(0, 2)
        def _(c):
            rows = pl.ds(pl.multiple_of(c * 256, 256), 256)
            out_ref[rows, :] = parent_ref[rows, :] - mm_nt(p_buf[0, rows, :], p_buf[1])
        done = t_buf.at[pl.ds(0, 480)]
        pltpu.make_async_copy(done, done, dist_recv.at[0]).wait()

    @pl.when(jnp.logical_and(trail, ci >= cj))
    def _():
        out_ref[...] = out_ref[...] - t_buf[...]

    @pl.when(jnp.logical_and(trail, ci < cj))
    def _():
        for b in range(4):
            o = b * BLK
            out_ref[:, o:o + BLK] = out_ref[:, o:o + BLK] - t_buf[o:o + BLK, :].T

    @pl.when(jnp.logical_and(ci > 0, cj == 0))
    def _():
        out_ref[...] = p_buf[0]

    @pl.when(jnp.logical_and(ci == 0, cj == 0))
    def _():
        out_ref[...] = ch[...]

    @pl.when(jnp.logical_and(ci == 0, cj > 0))
    def _():
        for c in range(2):
            for a in range(2):
                o = c * 256 + a * 128
                v = jnp.reshape(w_buf[c, 2 * a:2 * a + 2, pl.ds(cj, 1)], (BLK, TILE))
                out_ref[:, o:o + BLK] = -(v.T)

    for cp in started:
        cp.wait_send()
    for mine, cp in deliveries:
        @pl.when(jnp.logical_not(mine))
        def _():
            cp.wait_send()


def body(child_inverse, child_coupling, child_blocks, child_map, parent_front):
    ids = jnp.arange(16)[:, None]
    slots = jnp.arange(8)[None, :]
    hit = jnp.logical_and(child_map[0][None, :] == ids, slots < child_blocks[0])
    slot = jnp.concatenate([jnp.sum(jnp.where(hit, slots, 0), axis=1), jnp.any(hit, axis=1).astype(jnp.int32)]).astype(jnp.int32)
    vm = pltpu.VMEM
    dma = pltpu.SemaphoreType.DMA
    return pl.pallas_call(
        kernel,
        out_shape=jax.ShapeDtypeStruct((TILE, TILE), F32),
        in_specs=[pl.BlockSpec(memory_space=pltpu.SMEM)] + [pl.BlockSpec(memory_space=vm)] * 3,
        out_specs=pl.BlockSpec(memory_space=vm),
        scratch_shapes=[
            vm((8, BLK, TILE), BF16), vm((8, BLK, TILE), BF16),
            vm((2048, TILE), BF16), vm((2048, TILE), BF16),
            vm((2, 4, NT, 64, TILE), F32),
            vm((2, 2, NT, 32, TILE), F32), vm((2, 2, NT, 64, TILE), F32),
            vm((2, 2, NT, 8, TILE), F32), vm((2, 2, NT, 16, TILE), F32),
            vm((2, 4, 4, 64, TILE), F32), vm((2, 6, 16, TILE), F32), vm((TILE, TILE), F32),
            vm((TILE, TILE), F32), vm((BLK, 2 * BLK), F32), vm((4, BLK, BLK), F32), vm((2, TILE, TILE), F32),
            dma((4, 2, 2, 10)), dma((4, 2, 2, 10)), dma((6, 2, 2)), dma((1,)),
        ],
        compiler_params=pltpu.CompilerParams(collective_id=0, has_side_effects=True, vmem_limit_bytes=60 * 1024 * 1024),
    )(slot, child_inverse[0], child_coupling[0], parent_front)


def solution(mesh):
    return jax.shard_map(
        body,
        mesh=mesh,
        in_specs=(
            P(("leaf", "prow", "pcol"), None, None),
            P(("leaf", "prow", "pcol"), None, None),
            P(("leaf", "prow", "pcol")),
            P(("leaf", "prow", "pcol"), None),
            P(("leaf", "prow"), "pcol"),
        ),
        out_specs=P(("leaf", "prow"), "pcol"),
        check_vma=False,
    )
```

time: 493 us -> 147 us (0.30)
  the two profiles are of different devices: /device:TPU:1 before, /device:TPU:246 now
where the time goes in v1:
time: 147 us; the launch traced here: 146 us
  Pallas kernels  141 us (96%)
  local copies, waits for them, and re-layouts  2.26 us (2%)
  other arithmetic  2.08 us (1%)
    pallas_call x1, Pallas kernels, body(): pl.pallas_call(kernel, out_shape=jax.ShapeDtypeStruct((TILE, TILE), F32),...  141 us

profile of v1, /device:TPU:246, one launch (start us, length us, event | category | flops | bytes accessed | tf_op | source)
XLA Modules:
  0.0 146.0 jit_solution(16774526843999067323)
XLA Ops:
  0.7 0.7 fusion.1
  1.4 0.7 select_reduce_fusion
  2.2 0.6 pad_add_fusion.slot_ref
  2.7 141.0 %shard_map.55 = f32[512,512]{1,0:T(8,128)} custom-call(s32[32]{0:T(128)} %pad_add_fusion.slot_ref, f32[512,512]{1,0:T(8,128)} %bitcast.6, f32[1024,512]{1,0:T(8,128)} %bitcast.5, f32[512,512]{1,0:T(8,128)} %parent_ref.1), custom_call_target="tpu_custom_call" | custom-call | tf_op jit(solution)/shard_map/pallas_call | solution.py:411
  143.7 2.3 %copy.8 = f32[512,512]{1,0:T(8,128)} copy(f32[512,512]{1,0:T(8,128)} %shard_map.55) | data formatting | bytes 2097152
  (2 shorter events, 0.0 us)

commit v2 on v0

v2 whole, which is shorter than its diff:
```python
import functools

import jax
import jax.numpy as jnp
from jax import lax
from jax.experimental import pallas as pl
from jax.experimental.pallas import tpu as pltpu
from jax.sharding import PartitionSpec as P

BLK = 128
TILE = 512
NT = 10
PACK = (384, 256)
DIAG = (0, 4, 7, 9)
OWNERS = ((1, 1), (2, 1), (3, 1), (2, 2), (3, 2), (3, 3))
AXES = ("prow", "pcol")
F32 = jnp.float32
BF16 = jnp.bfloat16
DN_NT = (((1,), (1,)), ((), ()))


def split(x):
    hi = x.astype(BF16)
    return hi, (x - hi.astype(F32)).astype(BF16)


def dot_nt(a, b):
    return lax.dot_general(a, b, DN_NT, preferred_element_type=F32)


def dot3(a, b):
    return dot_nt(a[0], b[0]) + dot_nt(a[0], b[1]) + dot_nt(a[1], b[0])


def mm_nt(a, b):
    return dot3(split(a), split(b))


def kernel(map_ref, blocks_ref, inv_ref, coup_ref, parent_ref, out_ref,
           fac_h, fac_l, fh, fl, s_buf, rl1, rf1, rf2, g1, g2, w0, wr, wc, z_buf, t_buf,
           ch, md, linv, p_buf,
           send_sem, recv_sem, send2_sem, recv2_sem, xs_sem, xr_sem, pa_send, pa_recv, pb_send, pb_recv, dist_send, dist_recv):
    ci = lax.axis_index("prow")
    cj = lax.axis_index("pcol")
    coord = {"prow": ci, "pcol": cj}
    mesh_id = pl.DeviceIdType.MESH

    def nxt(v, k):
        return lax.rem(v + k, 4)

    def width(t, c):
        return PACK[c] if t in DIAG else TILE

    barrier = pltpu.get_barrier_semaphore()
    for dx in range(4):
        for dy in range(4):
            if dx or dy:
                pl.semaphore_signal(
                    barrier, inc=1,
                    device_id={"prow": nxt(ci, dx), "pcol": nxt(cj, dy)},
                    device_id_type=mesh_id)

    ih, il = split(inv_ref[...])

    @pl.loop(0, 8)
    def _(s):
        c = split(coup_ref[pl.ds(pl.multiple_of(s * BLK, BLK), BLK), :])
        f = dot3(c, (ih, il))
        h, l = split(f)
        fac_h[s] = h
        fac_l[s] = l

    def place(b):
        s = jnp.int32(0)
        found = jnp.int32(0)
        for k in range(8):
            hit = jnp.logical_and(map_ref[0, k] == b, blocks_ref[0] > k)
            s = jnp.where(hit, k, s)
            found = jnp.where(hit, 1, found)
        h = fac_h[s]
        l = fac_l[s]
        rows = pl.ds(pl.multiple_of(b * BLK, BLK), BLK)
        fh[rows, :] = jnp.where(found > 0, h, jnp.zeros_like(h))
        fl[rows, :] = jnp.where(found > 0, l, jnp.zeros_like(l))

    pl.loop(0, 4)(place)

    def tiles(col, lo, hi, base):
        @pl.loop(lo, hi)
        def _(r):
            rows = pl.ds(pl.multiple_of(r * TILE, TILE), TILE)
            cols = pl.ds(col * TILE, TILE)
            d = dot3((fh[rows, :], fl[rows, :]), (fh[cols, :], fl[cols, :]))
            if col == 0:
                mine = jnp.logical_and(ci == r, cj == 0)
                d = d - jnp.where(mine, parent_ref[...], jnp.zeros((TILE, TILE), F32))
            for c in range(2):
                for a in range(4):
                    o = c * 256 + a * 64
                    s_buf[c, a, base + r] = d[o:o + 64]
        if lo == col:
            t = base + col
            for a in range(2):
                s_buf[0, a, t, :, 256:384] = s_buf[1, a, t, :, 256:384]
                s_buf[0, a, t, :, 128:256] = s_buf[1, 2 + a, t, :, 384:512]
                s_buf[0, 2 + a, t, :, 256:384] = s_buf[1, 2 + a, t, :, 256:384]

    def remote(src, dst, ss, rs_, dev):
        return functools.partial(
            pltpu.make_async_remote_copy, src_ref=src, dst_ref=dst, send_sem=ss, recv_sem=rs_,
            device_id=dev, device_id_type=mesh_id)

    started = []

    def go(cp):
        cp().start()
        started.append(cp)

    STEP = (1, 3)

    def x_copy(stage, c, k, src, dst, axis):
        return remote(src, dst, xs_sem.at[stage, c, k - 1], xr_sem.at[stage, c, k - 1], {axis: nxt(coord[axis], k)})

    def x_list(stage):
        out = []
        for k in (2, 1, 3):
            for c in range(2):
                cols = pl.ds(0, PACK[c])
                m, n = coord[AXES[c]], coord[AXES[1 - c]]
                if stage == 0:
                    out.append(x_copy(0, c, k, s_buf.at[c, nxt(m, k), 0, :, cols], g1.at[c, k - 1, :, cols], AXES[c]))
                elif stage == 1:
                    rows = pl.ds(pl.multiple_of(nxt(n, k) * 16, 16), 16)
                    out.append(x_copy(1, c, k, s_buf.at[c, m, 0, rows, cols], g2.at[c, k - 1, :, cols], AXES[1 - c]))
                else:
                    if stage == 2:
                        ref, axis = w0.at[c, m, pl.ds(pl.multiple_of(n * 16, 16), 16), cols], AXES[1 - c]
                    else:
                        ref, axis = w0.at[c, m, :, cols], AXES[c]
                    out.append(x_copy(stage, c, k, ref, ref, axis))
        return out

    def x_start(stage):
        for cp in x_list(stage):
            go(cp)

    def x_wait(stage):
        for cp in x_list(stage):
            cp().wait_recv()
        for c in range(2):
            m, n = coord[AXES[c]], coord[AXES[1 - c]]
            w = PACK[c]
            if stage == 0:
                s_buf[c, m, 0, :, 0:w] = ((s_buf[c, m, 0, :, 0:w] + g1[c, 0, :, 0:w])
                                          + (g1[c, 1, :, 0:w] + g1[c, 2, :, 0:w]))
            elif stage == 1:
                rows = pl.ds(pl.multiple_of(n * 16, 16), 16)
                w0[c, m, rows, 0:w] = ((s_buf[c, m, 0, rows, 0:w] + g2[c, 0, :, 0:w])
                                       + (g2[c, 1, :, 0:w] + g2[c, 2, :, 0:w]))

    def rs(t, c):
        cols = pl.ds(0, width(t, c))
        axis = AXES[c]
        me = coord[axis]

        def chunk(d, h):
            return s_buf.at[c, d, t, pl.ds(h * 32, 32), cols]

        def mk(kind, src, dst, d):
            return remote(src, dst, send_sem.at[t - 1, c, d, kind], recv_sem.at[t - 1, c, d, kind],
                          {axis: nxt(me, STEP[d])})
        relay = [mk(0, chunk(nxt(me, 2), 1 - d), rl1.at[c, d, t, :, cols], d) for d in range(2)]
        raw = [mk(1, chunk(nxt(me, STEP[d]), d), rf1.at[c, d, t, pl.ds(d * 32, 32), cols], d) for d in range(2)]
        fin = [mk(2, chunk(nxt(me, STEP[d]), 1 - d), rf1.at[c, d, t, pl.ds((1 - d) * 32, 32), cols], d)
               for d in range(2)]
        return relay, raw, fin, chunk, me

    def second(t):
        out = []
        for k in (2, 1, 3):
            for c in range(2):
                cols = pl.ds(0, width(t, c))
                m, n = coord[AXES[c]], coord[AXES[1 - c]]
                rows = pl.ds(pl.multiple_of(nxt(n, k) * 16, 16), 16)
                out.append(remote(s_buf.at[c, m, t, rows, cols], rf2.at[c, k - 1, t, :, cols],
                                  send2_sem.at[t - 1, c, k - 1], recv2_sem.at[t - 1, c, k - 1],
                                  {AXES[1 - c]: nxt(n, k)}))
        return out

    def ev_a(t):
        for c in range(2):
            relay, raw = rs(t, c)[:2]
            for d in range(2):
                go(relay[d])
            for d in range(2):
                go(raw[d])

    def ev_b(t):
        for c in range(2):
            relay, raw, fin, chunk, me = rs(t, c)
            for d in range(2):
                relay[d]().wait_recv()
                ref = chunk(nxt(me, STEP[d]), 1 - d)
                ref[...] = ref[...] + rl1[c, d, t, :, 0:width(t, c)]
                go(fin[d])

    def ev_c(t):
        for c in range(2):
            w = width(t, c)
            relay, raw, fin, chunk, me = rs(t, c)
            for d in range(2):
                raw[d]().wait_recv()
                fin[d]().wait_recv()
            m = coord[AXES[c]]
            s_buf[c, m, t, :, 0:w] = s_buf[c, m, t, :, 0:w] + rf1[c, 0, t, :, 0:w] + rf1[c, 1, t, :, 0:w]
        for cp in second(t):
            go(cp)

    def ev_e(t):
        for cp in second(t):
            cp().wait_recv()
        for c in range(2):
            w = width(t, c)
            m, n = coord[AXES[c]], coord[AXES[1 - c]]
            rows = pl.ds(pl.multiple_of(n * 16, 16), 16)
            z_buf[c, t - 1, :, 0:w] = ((s_buf[c, m, t, rows, 0:w] + rf2[c, 0, t, :, 0:w])
                                       + (rf2[c, 1, t, :, 0:w] + rf2[c, 2, t, :, 0:w]))
        if t < 4:
            panel_send(t)
        else:
            deliver(t)

    guarded = []

    def go_unless(mine, cp):
        @pl.when(jnp.logical_not(mine))
        def _():
            cp().start()
        guarded.append((jnp.logical_not(mine), cp))

    def panel_send(t):
        for c in range(2):
            m, n = coord[AXES[c]], coord[AXES[1 - c]]
            rows = pl.ds(pl.multiple_of(n * 16, 16), 16)
            for k, (buf, axis) in enumerate(((wr, "prow"), (wc, "pcol"))):
                mine = coord[axis] == t

                @pl.when(mine)
                def _():
                    buf[c, m, rows, :] = z_buf[c, t - 1]
                go_unless(mine, remote(z_buf.at[c, t - 1], buf.at[c, m, rows], pa_send.at[t - 1, c, k], pa_recv.at[k], {axis: t}))

    def ring(k):
        buf, axis = ((wr, "pcol"), (wc, "prow"))[k]
        me = coord[axis]

        def part(v, c, h, n):
            if c != k:
                return buf.at[c, v, pl.ds(h * 32, n * 32)]
            return buf.at[c, pl.ds(h * 2, n * 2), pl.ds(pl.multiple_of(v * 16, 16), 16)]
        res = []
        for c in range(2):
            for d in range(2):
                def mk(kind, ref):
                    return remote(ref, ref, pb_send.at[k, c, d, kind], pb_recv.at[k, c, d, kind], {axis: nxt(me, STEP[d])})
                prev = nxt(me, STEP[1 - d])
                res.append((mk(0, part(me, c, 0, 2)), mk(0, part(prev, c, 0, 2)),
                            mk(1, part(prev, c, d, 1)), mk(1, part(nxt(me, 2), c, d, 1))))
        return res

    def panel_stage(stage):
        for k in range(2):
            @pl.when((ci, cj)[k] > 0)
            def _():
                if stage == 0:
                    got = (wr, wc)[k].at[0, pl.ds(0, 3), pl.ds(0, 32)]
                    pltpu.make_async_copy(got, got, pa_recv.at[k]).wait()
                for own, own_in, fwd, fwd_in in ring(k):
                    if stage == 0:
                        own().start()
                    elif stage == 1:
                        own_in().wait_recv()
                        fwd().start()
                    elif stage == 2:
                        fwd_in().wait_recv()
                    else:
                        own().wait_send()
                        fwd().wait_send()

    def deliver(t):
        r, q = OWNERS[t - 4]
        for k, (x, y) in enumerate(((r, q), (q, r))[: 1 if r == q else 2]):
            mine = jnp.logical_and(ci == x, cj == y)
            for c in range(2):
                cols = pl.ds(0, width(t, c))
                m, v = coord[AXES[c]], coord[AXES[1 - c]]
                rows = pl.ds(pl.multiple_of(c * 256 + m * 64 + v * 16, 16), 16)

                @pl.when(mine)
                def _():
                    t_buf[rows, cols] = z_buf[c, t - 1, :, cols]
                go_unless(mine, remote(z_buf.at[c, t - 1, :, cols], t_buf.at[rows, cols], dist_send.at[t - 4, k, c],
                                       dist_recv.at[0], {"prow": x, "pcol": y}))

    def chol_begin(kb):
        o = kb * BLK
        eye = lax.broadcasted_iota(jnp.int32, (BLK, BLK), 0) == lax.broadcasted_iota(jnp.int32, (BLK, BLK), 1)
        md[:, 0:BLK] = ch[o:o + BLK, o:o + BLK]
        md[:, BLK:2 * BLK] = eye.astype(F32)

    def chol_chunk(q):
        lo = q * 32
        x = md[lo:BLK, 0:BLK]
        y = md[lo:BLK, BLK:2 * BLK]
        rid = lax.broadcasted_iota(jnp.int32, (BLK - lo, BLK), 0)
        for k in range(0, 32, 2):
            c0 = jnp.broadcast_to(x[:, lo + k:lo + k + 1], x.shape)
            c1 = jnp.broadcast_to(x[:, lo + k + 1:lo + k + 2], x.shape)
            a = c0[k:k + 1, :]
            b = c0[k + 1:k + 2, :]
            d = c1[k + 1:k + 2, :]
            ia = 1.0 / a
            ba = b * ia
            s = d - b * ba
            isv = 1.0 / s
            m0 = jnp.where(rid > k + 1, c0, 0.0)
            m1 = jnp.where(rid > k + 1, c1, 0.0) - m0 * ba
            m0 = jnp.where(rid == k + 1, b, m0)
            xa = x[k:k + 1, :]
            ya = y[k:k + 1, :]
            xb = (x[k + 1:k + 2, :] - ba * xa) * isv
            yb = (y[k + 1:k + 2, :] - ba * ya) * isv
            xa = xa * ia
            ya = ya * ia
            x = x - m0 * xa - m1 * xb
            y = y - m0 * ya - m1 * yb
        md[lo:BLK, 0:BLK] = x
        md[lo:BLK, BLK:2 * BLK] = y

    def chol_end(kb):
        o = kb * BLK
        ri = lax.broadcasted_iota(jnp.int32, (BLK, BLK), 0)
        cj_ = lax.broadcasted_iota(jnp.int32, (BLK, BLK), 1)
        u = md[:, 0:BLK]
        piv = jnp.sum(jnp.where(ri == cj_, u, 0.0), axis=1, keepdims=True)
        sc = lax.rsqrt(piv)
        li = md[:, BLK:2 * BLK] * sc
        linv[kb] = li
        low = jnp.where(cj_ >= ri, u * sc, 0.0).T
        ch[o:o + BLK, o:o + BLK] = low
        if kb < 3:
            lp = lax.dot_general(ch[o + BLK:, o:o + BLK], li, DN_NT, precision=lax.Precision.HIGHEST,
                                 preferred_element_type=F32)
            ch[o + BLK:, o:o + BLK] = lp
            ch[o + BLK:, o + BLK:] = ch[o + BLK:, o + BLK:] - lax.dot_general(
                lp, lp, DN_NT, precision=lax.Precision.HIGHEST, preferred_element_type=F32)
            ch[o:o + BLK, o + BLK:] = jnp.zeros((BLK, TILE - o - BLK), F32)

    def solve(x, buf):
        @pl.loop(0, 2)
        def _(c):
            a = -jnp.reshape(buf[c], (256, TILE))
            rows = pl.ds(pl.multiple_of(c * 256, 256), 256)
            for b in range(4):
                o = b * BLK
                v = a[:, o:o + BLK]
                if b:
                    v = v - mm_nt(p_buf[x, rows, 0:o], ch[o:o + BLK, 0:o])
                p_buf[x, rows, o:o + BLK] = mm_nt(v, linv[b])

    tiles(0, 0, 1, 0)
    pl.semaphore_wait(barrier, 15)
    x_start(0)
    pl.loop(4, 16)(place)
    tiles(0, 1, 4, 0)
    ev_a(1)
    x_wait(0)
    x_start(1)
    ev_a(2)
    tiles(1, 1, 4, 3)
    x_wait(1)
    x_start(2)
    ev_b(1)
    ev_a(3)
    x_wait(2)
    x_start(3)
    ev_b(2)
    ev_a(4)
    tiles(2, 2, 4, 5)
    tiles(3, 3, 4, 6)
    ev_c(1)

    fn = {"a": ev_a, "b": ev_b, "c": ev_c, "e": ev_e, "p": panel_stage}
    order = ("b3 a5 c2", "e1 b4 a6", "c3 e2 b5", "a7 c4 e3", "b6 a8 c5", "p0 e4 b7", "a9 c6 p1", "e5 b8 c7",
             "p2 e6 b9", "c8 e7 c9", "e8 e9")
    order = [w for part in order for w in part.split()]
    head = 28
    x_wait(3)
    ch[...] = jnp.zeros((TILE, TILE), F32)
    for a in range(4):
        o = a * 64
        n = 128 * (1 + a // 2)
        ch[o:o + 64, 0:n] = -w0[0, a, :, 0:n]
        ch[256 + o:320 + o, 0:256] = -w0[1, a, :, 0:256]
        ch[256 + o:320 + o, 256:384] = -w0[0, a, :, 256:384]
    for a in range(2):
        ch[384 + a * 64:448 + a * 64, 384:512] = -w0[0, a, :, 128:256]

    at = 0
    for kb in range(4):
        chol_begin(kb)
        for q in range(4):
            upto = (head * (4 * kb + q + 1)) // 16
            while at < upto:
                fn[order[at][0]](int(order[at][1]))
                at += 1
            chol_chunk(q)
        chol_end(kb)

    trail = jnp.logical_and(ci > 0, cj > 0)
    for n, w in enumerate(order[head:]):
        fn[w[0]](int(w[1]))
        if n == 1:
            @pl.when(ci > 0)
            def _():
                solve(0, wr)
        if n == 3:
            @pl.when(trail)
            def _():
                solve(1, wc)

                @pl.loop(0, 2)
                def _(c):
                    rows = pl.ds(pl.multiple_of(c * 256, 256), 256)
                    out_ref[rows, :] = parent_ref[rows, :] - mm_nt(p_buf[0, rows, :], p_buf[1])

    def arrived(rows, w):
        done = t_buf.at[pl.ds(0, rows), pl.ds(0, w)]
        pltpu.make_async_copy(done, done, dist_recv.at[0]).wait()

    @pl.when(jnp.logical_and(trail, ci == cj))
    def _():
        arrived(400, 384)
        for p in range(4):
            for q in range(p + 1):
                y, x = {(2, 2): (0, 2), (3, 2): (1, 2), (3, 3): (0, 1)}.get((p, q), (p, q))
                v = t_buf[y * BLK:(y + 1) * BLK, x * BLK:(x + 1) * BLK]
                out_ref[p * BLK:(p + 1) * BLK, q * BLK:(q + 1) * BLK] -= v
                if p != q:
                    out_ref[q * BLK:(q + 1) * BLK, p * BLK:(p + 1) * BLK] -= v.T

    @pl.when(jnp.logical_and(trail, ci > cj))
    def _():
        arrived(480, TILE)
        out_ref[...] = out_ref[...] - t_buf[...]

    @pl.when(jnp.logical_and(trail, ci < cj))
    def _():
        arrived(480, TILE)
        for b in range(4):
            o = b * BLK
            out_ref[:, o:o + BLK] = out_ref[:, o:o + BLK] - t_buf[o:o + BLK, :].T

    @pl.when(jnp.logical_and(ci > 0, cj == 0))
    def _():
        out_ref[...] = p_buf[0]

    @pl.when(jnp.logical_and(ci == 0, cj == 0))
    def _():
        out_ref[...] = ch[...]

    @pl.when(jnp.logical_and(ci == 0, cj > 0))
    def _():
        for c in range(2):
            for a in range(2):
                o = c * 256 + a * 128
                out_ref[:, o:o + BLK] = -(jnp.reshape(wc[c, 2 * a:2 * a + 2], (BLK, TILE)).T)

    for cp in started:
        cp().wait_send()
    panel_stage(3)
    for cond, cp in guarded:
        @pl.when(cond)
        def _():
            cp().wait_send()


def body(child_inverse, child_coupling, child_blocks, child_map, parent_front):
    vm = pltpu.VMEM
    dma = pltpu.SemaphoreType.DMA
    return pl.pallas_call(
        kernel,
        out_shape=jax.ShapeDtypeStruct((TILE, TILE), F32),
        in_specs=[pl.BlockSpec(memory_space=pltpu.SMEM)] * 2 + [pl.BlockSpec(memory_space=vm)] * 3,
        out_specs=pl.BlockSpec(memory_space=vm),
        scratch_shapes=[
            vm((8, BLK, TILE), BF16), vm((8, BLK, TILE), BF16),
            vm((2048, TILE), BF16), vm((2048, TILE), BF16),
            vm((2, 4, NT, 64, TILE), F32),
            vm((2, 2, NT, 32, TILE), F32), vm((2, 2, NT, 64, TILE), F32),
            vm((2, 3, NT, 16, TILE), F32),
            vm((2, 3, 64, 384), F32), vm((2, 3, 16, 384), F32), vm((2, 4, 64, 384), F32),
            vm((2, 4, 64, TILE), F32), vm((2, 4, 64, TILE), F32),
            vm((2, 9, 16, TILE), F32), vm((TILE, TILE), F32),
            vm((TILE, TILE), F32), vm((BLK, 2 * BLK), F32), vm((4, BLK, BLK), F32), vm((2, TILE, TILE), F32),
            dma((9, 2, 2, 3)), dma((9, 2, 2, 3)), dma((9, 2, 3)), dma((9, 2, 3)), dma((4, 2, 3)), dma((4, 2, 3)),
            dma((3, 2, 2)), dma((2,)), dma((2, 2, 2, 2)), dma((2, 2, 2, 2)), dma((6, 2, 2)), dma((1,)),
        ],
        compiler_params=pltpu.CompilerParams(collective_id=0, has_side_effects=True, vmem_limit_bytes=46 * 1024 * 1024),
    )(child_map, child_blocks, child_inverse[0], child_coupling[0], parent_front)


def solution(mesh):
    return jax.shard_map(
        body,
        mesh=mesh,
        in_specs=(
            P(("leaf", "prow", "pcol"), None, None),
            P(("leaf", "prow", "pcol"), None, None),
            P(("leaf", "prow", "pcol")),
            P(("leaf", "prow", "pcol"), None),
            P(("leaf", "prow"), "pcol"),
        ),
        out_specs=P(("leaf", "prow"), "pcol"),
        check_vma=False,
    )
```

time: 493 us -> 109 us (0.22)
  the two profiles are of different devices: /device:TPU:1 before, /device:TPU:246 now
where the time goes in v2:
time: 109 us
  Pallas kernels  102 us (94%)
  local copies, waits for them, and re-layouts  5.66 us (5%)
    pallas_call x1, Pallas kernels, body(): pl.pallas_call(kernel, out_shape=jax.ShapeDtypeStruct((TILE, TILE), F32),...  102 us
    unnamed x9, local copies, waits for them, and re-layouts  5.66 us

profile of v2, /device:TPU:246, one launch (start us, length us, event | category | flops | bytes accessed | tf_op | source)
XLA Modules:
  0.0 108.7 jit_solution(10914052371833211710)
XLA Ops:
  0.7 0.0 copy-start
  0.7 1.6 %copy-done = f32[1,1024,512]{2,1,0:T(8,128)S(1)} copy-done((f32[1,1024,512]{2,1,0:T(8,128)S(1)}, f32[1,1024,512]{2,1,0:T(8,128)}, u32[]{:S(2)}) %copy-start) | copy-done | bytes 2097176
  2.2 0.0 copy-start.1
  2.2 1.2 %copy-done.1 = f32[1,512,512]{2,1,0:T(8,128)S(1)} copy-done((f32[1,512,512]{2,1,0:T(8,128)S(1)}, f32[1,512,512]{2,1,0:T(8,128)}, u32[]{:S(2)}) %copy-start.1) | copy-done | bytes 1048600
  3.5 0.0 copy-start.2
  3.5 1.2 %copy-done.2 = f32[512,512]{1,0:T(8,128)S(1)} copy-done((f32[512,512]{1,0:T(8,128)S(1)}, f32[512,512]{1,0:T(8,128)}, u32[]{:S(2)}) %copy-start.2) | copy-done | bytes 1048600
  4.7 0.0 copy-start.3
  4.7 0.7 copy-done.3
  5.4 102.4 %shard_map.55 = f32[512,512]{1,0:T(8,128)S(1)} custom-call(s32[1,8]{1,0:T(1,128)S(1)} %copy-done.3, s32[1]{0:T(128)S(6)} %copy.7.blocks_ref, f32[512,512]{1,0:T(8,128)S(1)} %bitcast.3, f32[1024,512]{1,0:T(8,128)S(1)} %bitcast.2, f32[512,512]{1,0:T(8,128)S(1)} %copy-done.2), custom_call_target="tpu_custom_call" | custom-call | tf_op jit(solution)/shard_map/pallas_call | solution.py:491
  107.7 1.0 copy.8
Async XLA Ops:
  0.7 1.6 %copy-start = (f32[1,1024,512]{2,1,0:T(8,128)S(1)}, f32[1,1024,512]{2,1,0:T(8,128)}, u32[]{:S(2)}) copy-start(f32[1,1024,512]{2,1,0:T(8,128)} %param.6) | copy-start | bytes 6291460
  2.2 1.2 %copy-start.1 = (f32[1,512,512]{2,1,0:T(8,128)S(1)}, f32[1,512,512]{2,1,0:T(8,128)}, u32[]{:S(2)}) copy-start(f32[1,512,512]{2,1,0:T(8,128)} %param.5) | copy-start | bytes 3145732
  3.5 1.2 %copy-start.2 = (f32[512,512]{1,0:T(8,128)S(1)}, f32[512,512]{1,0:T(8,128)}, u32[]{:S(2)}) copy-start(f32[512,512]{1,0:T(8,128)} %parent_ref.1) | copy-start | bytes 3145732
  4.7 0.7 copy-start.3

commit v3 on v2

--- a/solution.py
+++ b/solution.py
@@ -36,7 +36,8 @@
     return dot3(split(a), split(b))
 
 
-def kernel(map_ref, blocks_ref, inv_ref, coup_ref, parent_ref, out_ref,
+def kernel(map_hbm, blocks_ref, inv_hbm, coup_hbm, parent_hbm, out_ref,
+           map_ref, inv_ref, coup_ref, parent_ref, in_sem,
            fac_h, fac_l, fh, fl, s_buf, rl1, rf1, rf2, g1, g2, w0, wr, wc, z_buf, t_buf,
            ch, md, linv, p_buf,
            send_sem, recv_sem, send2_sem, recv2_sem, xs_sem, xr_sem, pa_send, pa_recv, pb_send, pb_recv, dist_send, dist_recv):
@@ -50,6 +51,18 @@
 
     def width(t, c):
         return PACK[c] if t in DIAG else TILE
+
+    load_inv = pltpu.make_async_copy(inv_hbm, inv_ref, in_sem.at[0])
+    load_inv.start()
+    load_map = pltpu.make_async_copy(map_hbm, map_ref, in_sem.at[1])
+    loads = []
+    for s in range(4):
+        rows = pl.ds(s * 256, 256)
+        loads.append(pltpu.make_async_copy(coup_hbm.at[rows], coup_ref.at[rows], in_sem.at[3 + s]))
+        loads[s].start()
+    load_map.start()
+    load_parent = pltpu.make_async_copy(parent_hbm, parent_ref, in_sem.at[2])
+    load_parent.start()
 
     barrier = pltpu.get_barrier_semaphore()
     for dx in range(4):
@@ -60,15 +73,17 @@
                     device_id={"prow": nxt(ci, dx), "pcol": nxt(cj, dy)},
                     device_id_type=mesh_id)
 
+    load_inv.wait()
     ih, il = split(inv_ref[...])
-
-    @pl.loop(0, 8)
-    def _(s):
-        c = split(coup_ref[pl.ds(pl.multiple_of(s * BLK, BLK), BLK), :])
-        f = dot3(c, (ih, il))
-        h, l = split(f)
-        fac_h[s] = h
-        fac_l[s] = l
+    for s in range(4):
+        loads[s].wait()
+        c = split(coup_ref[s * 256:s * 256 + 256, :])
+        h, l = split(dot3(c, (ih, il)))
+        for k in range(2):
+            fac_h[2 * s + k] = h[k * BLK:k * BLK + BLK]
+            fac_l[2 * s + k] = l[k * BLK:k * BLK + BLK]
+    load_map.wait()
+    load_parent.wait()
 
     def place(b):
         s = jnp.int32(0)
@@ -491,9 +506,10 @@
     return pl.pallas_call(
         kernel,
         out_shape=jax.ShapeDtypeStruct((TILE, TILE), F32),
-        in_specs=[pl.BlockSpec(memory_space=pltpu.SMEM)] * 2 + [pl.BlockSpec(memory_space=vm)] * 3,
+        in_specs=[pl.BlockSpec(memory_space=pltpu.SMEM if k == 1 else pltpu.HBM) for k in range(5)],
         out_specs=pl.BlockSpec(memory_space=vm),
         scratch_shapes=[
+            pltpu.SMEM((1, 8), jnp.int32), vm((TILE, TILE), F32), vm((1024, TILE), F32), vm((TILE, TILE), F32), dma((7,)),
             vm((8, BLK, TILE), BF16), vm((8, BLK, TILE), BF16),
             vm((2048, TILE), BF16), vm((2048, TILE), BF16),
             vm((2, 4, NT, 64, TILE), F32),
@@ -506,7 +522,7 @@
             dma((9, 2, 2, 3)), dma((9, 2, 2, 3)), dma((9, 2, 3)), dma((9, 2, 3)), dma((4, 2, 3)), dma((4, 2, 3)),
             dma((3, 2, 2)), dma((2,)), dma((2, 2, 2, 2)), dma((2, 2, 2, 2)), dma((6, 2, 2)), dma((1,)),
         ],
-        compiler_params=pltpu.CompilerParams(collective_id=0, has_side_effects=True, vmem_limit_bytes=46 * 1024 * 1024),
+        compiler_params=pltpu.CompilerParams(collective_id=0, has_side_effects=True, vmem_limit_bytes=60 * 1024 * 1024),
     )(child_map, child_blocks, child_inverse[0], child_coupling[0], parent_front)
 
 

time: 109 us -> 104 us (0.954)
  local copies, waits for them, and re-layouts: 5.66 us -> 2.26 us
    unnamed x9 -> x1, local copies, waits for them, and re-layouts: 5.66 us -> 2.26 us
where the time goes in v3:
time: 104 us
  Pallas kernels  101 us (97%)
  local copies, waits for them, and re-layouts  2.26 us (2%)
    pallas_call x1, Pallas kernels, body(): pl.pallas_call(kernel, out_shape=jax.ShapeDtypeStruct((TILE, TILE), F32),...  101 us
    unnamed x1, local copies, waits for them, and re-layouts  2.26 us

profile of v3, /device:TPU:246, one launch (start us, length us, event | category | flops | bytes accessed | tf_op | source)
XLA Modules:
  0.0 104.3 jit_solution(11640719141997069594)
XLA Ops:
  0.7 101.4 %shard_map.55 = f32[512,512]{1,0:T(8,128)} custom-call(s32[1,8]{1,0:T(1,128)} %map_hbm.1, s32[1]{0:T(128)S(6)} %copy.7.blocks_ref, f32[512,512]{1,0:T(8,128)} %bitcast.3, f32[1024,512]{1,0:T(8,128)} %bitcast.2, f32[512,512]{1,0:T(8,128)} %parent_hbm.1), custom_call_target="tpu_custom_call" | custom-call | tf_op jit(solution)/shard_map/pallas_call | solution.py:506
  102.0 2.3 %copy.8 = f32[512,512]{1,0:T(8,128)} copy(f32[512,512]{1,0:T(8,128)} %shard_map.55) | data formatting | bytes 2097152

commit v4 on v3

--- a/solution.py
+++ b/solution.py
@@ -40,7 +40,7 @@
            map_ref, inv_ref, coup_ref, parent_ref, in_sem,
            fac_h, fac_l, fh, fl, s_buf, rl1, rf1, rf2, g1, g2, w0, wr, wc, z_buf, t_buf,
            ch, md, linv, p_buf,
-           send_sem, recv_sem, send2_sem, recv2_sem, xs_sem, xr_sem, pa_send, pa_recv, pb_send, pb_recv, dist_send, dist_recv):
+           send_sem, recv_sem, send2_sem, recv2_sem, xs_sem, xr_sem, xf_send, xf_recv, pa_send, pa_recv, pb_send, pb_recv, dist_send, dist_recv):
     ci = lax.axis_index("prow")
     cj = lax.axis_index("pcol")
     coord = {"prow": ci, "pcol": cj}
@@ -138,7 +138,7 @@
 
     def x_list(stage):
         out = []
-        for k in (2, 1, 3):
+        for k in ((2, 1, 3) if stage < 3 else (1, 3)):
             for c in range(2):
                 cols = pl.ds(0, PACK[c])
                 m, n = coord[AXES[c]], coord[AXES[1 - c]]
@@ -158,6 +158,24 @@
     def x_start(stage):
         for cp in x_list(stage):
             go(cp)
+
+    def x_forward(c, d, v):
+        axis = AXES[c]
+        me = coord[axis]
+        ref = w0.at[c, nxt(me, v), pl.ds(d * 32, 32), pl.ds(0, PACK[c])]
+        return remote(ref, ref, xf_send.at[c, d], xf_recv.at[c, d], {axis: nxt(me, STEP[d])})
+
+    def x_relay():
+        for c in range(2):
+            for d in range(2):
+                x_copy(3, c, (1, 3)[d], *[w0.at[c, nxt(coord[AXES[c]], (3, 1)[d]), :, pl.ds(0, PACK[c])]] * 2,
+                       AXES[c])().wait_recv()
+                go(x_forward(c, d, (3, 1)[d]))
+
+    def x_last():
+        for c in range(2):
+            for d in range(2):
+                x_forward(c, d, 2)().wait_recv()
 
     def x_wait(stage):
         for cp in x_list(stage):
@@ -404,13 +422,16 @@
     tiles(2, 2, 4, 5)
     tiles(3, 3, 4, 6)
     ev_c(1)
+    x_relay()
 
     fn = {"a": ev_a, "b": ev_b, "c": ev_c, "e": ev_e, "p": panel_stage}
-    order = ("b3 a5 c2", "e1 b4 a6", "c3 e2 b5", "a7 c4 e3", "b6 a8 c5", "p0 e4 b7", "a9 c6 p1", "e5 b8 c7",
-             "p2 e6 b9", "c8 e7 c9", "e8 e9")
+    order = ("c2 e1 b4", "a6 c3 e2", "b5 a7 c4", "e3 b6 a8", "c5 p0 e4", "b7 a9 c6", "p1 e5 b8", "c7 p2 e6",
+             "b9 c8 e7", "c9 e8 e9")
     order = [w for part in order for w in part.split()]
-    head = 28
-    x_wait(3)
+    head = 26
+    ev_b(3)
+    ev_a(5)
+    x_last()
     ch[...] = jnp.zeros((TILE, TILE), F32)
     for a in range(4):
         o = a * 64
@@ -519,7 +540,7 @@
             vm((2, 4, 64, TILE), F32), vm((2, 4, 64, TILE), F32),
             vm((2, 9, 16, TILE), F32), vm((TILE, TILE), F32),
             vm((TILE, TILE), F32), vm((BLK, 2 * BLK), F32), vm((4, BLK, BLK), F32), vm((2, TILE, TILE), F32),
-            dma((9, 2, 2, 3)), dma((9, 2, 2, 3)), dma((9, 2, 3)), dma((9, 2, 3)), dma((4, 2, 3)), dma((4, 2, 3)),
+            dma((9, 2, 2, 3)), dma((9, 2, 2, 3)), dma((9, 2, 3)), dma((9, 2, 3)), dma((4, 2, 3)), dma((4, 2, 3)), dma((2, 2)), dma((2, 2)),
             dma((3, 2, 2)), dma((2,)), dma((2, 2, 2, 2)), dma((2, 2, 2, 2)), dma((6, 2, 2)), dma((1,)),
         ],
         compiler_params=pltpu.CompilerParams(collective_id=0, has_side_effects=True, vmem_limit_bytes=60 * 1024 * 1024),

time: 104 us -> 103 us (level)
    pallas_call x1, Pallas kernels: 101 us -> 100 us  [body(): pl.pallas_call(kernel, out_shape=jax.ShapeDtypeStruct((TILE, TILE), F32),...]
where the time goes in v4:
time: 103 us
  Pallas kernels  100 us (97%)
  local copies, waits for them, and re-layouts  2.26 us (2%)
    pallas_call x1, Pallas kernels, body(): pl.pallas_call(kernel, out_shape=jax.ShapeDtypeStruct((TILE, TILE), F32),...  100 us
    unnamed x1, local copies, waits for them, and re-layouts  2.26 us

profile of v4, /device:TPU:246, one launch (start us, length us, event | category | flops | bytes accessed | tf_op | source)
XLA Modules:
  0.0 103.0 jit_solution(3307259993360309721)
XLA Ops:
  0.7 100.0 %shard_map.55 = f32[512,512]{1,0:T(8,128)} custom-call(s32[1,8]{1,0:T(1,128)} %map_hbm.1, s32[1]{0:T(128)S(6)} %copy.7.blocks_ref, f32[512,512]{1,0:T(8,128)} %bitcast.3, f32[1024,512]{1,0:T(8,128)} %bitcast.2, f32[512,512]{1,0:T(8,128)} %parent_hbm.1), custom_call_target="tpu_custom_call" | custom-call | tf_op jit(solution)/shard_map/pallas_call | solution.py:527
  100.7 2.3 %copy.8 = f32[512,512]{1,0:T(8,128)} copy(f32[512,512]{1,0:T(8,128)} %shard_map.55) | data formatting | bytes 2097152
